TPU v7x, 256 devices: a whole 4x4x8 slice. The times are simulated.
256 devices in a mesh: row: 16 (over x_lo, z), col: 16 (over x_hi, y, core).
Axes of the slice: x: 4 (x_hi: 2, x_lo: 2; x = x_hi * 2 + x_lo), y: 4, z: 8, core: 2. Of those that a mesh axis runs over, the one named last changes fastest.
Arguments:
- ham_blocks: bfloat16 [128, 4, 128, 128], P('row'), may hold values from -0.25 to 0.25
- ham_index: int32 [128, 4], P('row'), may hold values from -1 to 127, as said below
- coef_blocks: bfloat16 [64, 16, 128, 128], P('col', 'row'), may hold values from -0.5 to 0.5
- coef_index: int32 [64, 16], P('col', 'row'), may hold values from 0 to 127, as said below
- slab_blocks: bfloat16 [16, 16, 128, 128], P('row', 'col'), may hold values from -0.5 to 0.5
- slab_index: int32 [16, 16], P('row', 'col'), may hold values from 0 to 127, as said below
- pattern_index: int32 [16, 32], P('row', 'col'), may hold values from 0 to 63, as said below
Outputs:
- reduced_blocks: bfloat16 [16, 32, 128, 128], P('row', 'col')
Inputs may be any that keep to these rules, and one draw needn't show every extreme that they name: `ham_index`: each row lists its stored block columns first, all distinct, then -1 in every unused slot; a row holds 1 to 4 stored blocks, some row holds 4 and some row only one. `coef_index`: each row names 16 distinct orbital blocks. `slab_index`: each row names 16 distinct orbital blocks. `pattern_index`: entry k of a row names a block among (k // 2) * 4 to (k // 2) * 4 + 3.
All inputs are finite; a program needn't handle non-finite values.
Results may differ from a plain program's by a relative error of at most 0.0049.
Values may be sent and summed in bfloat16 or wider, within the bound.
No kernel may reach another device: no remote copies, remote signals or barrier semaphores. Data moves between devices by JAX's collectives and lax.ppermute only.
A program may use at most 128 MiB of HBM per device.

v0:
```python
import jax
import jax.numpy as jnp
from jax import lax
from jax.sharding import PartitionSpec as P


def panel_images(ham_part, index_part, column_vals, column_index):

    def one_row(row_item):
        block_row, index_row = row_item
        matches = (column_index[None, :, :] == index_row[:, None, None]).astype(jnp.bfloat16)
        columns = jnp.einsum(
            "kjm,jmab->kbja", matches, column_vals, preferred_element_type=jnp.float32
        ).astype(jnp.bfloat16)
        return jnp.einsum(
            "kxb,kbja->xja", block_row, columns, preferred_element_type=jnp.float32
        ).astype(jnp.bfloat16)

    row_total = ham_part.shape[0]
    return lax.map(one_row, (ham_part, index_part), batch_size=min(8, row_total))


def pick_image(where_row, wanted_row, products, offset):
    row_number = products.shape[0]
    targets = offset + jnp.arange(row_number, dtype=jnp.int32)
    matches = (where_row[:, None] == targets[None, :]).astype(jnp.bfloat16)
    columns = jnp.take(products, wanted_row, axis=2)
    return jnp.einsum("mn,nbkc->mbkc", matches, columns, preferred_element_type=jnp.float32)


def contract_row(coef_row, chosen):
    return jnp.einsum("mab,mbkc->kac", coef_row, chosen, preferred_element_type=jnp.float32)


def shards(ham_blocks, ham_index, coef_blocks, coef_index, slab_blocks, slab_index, pattern_index):
    column_vals, column_index = (
        lax.all_gather(coef_blocks, "row", axis=1, tiled=True),
        lax.all_gather(coef_index, "row", axis=1, tiled=True),
    )
    slab_vals, slab_where = (
        lax.all_gather(slab_blocks, "col", axis=1, tiled=True),
        lax.all_gather(slab_index, "col", axis=1, tiled=True),
    )
    col_blocks = coef_blocks.shape[0]
    block_size = coef_blocks.shape[2]
    column_pos = pattern_index - lax.axis_index("col") * col_blocks
    slab_count = slab_vals.shape[0]
    stored = slab_vals.shape[1]
    wanted_count = column_pos.shape[1]
    initial = jnp.zeros((slab_count, stored, block_size, wanted_count, block_size), jnp.float32)
    offset = jnp.int32(0)
    products = panel_images(
        lax.all_gather(ham_blocks, "row", axis=0, tiled=True),
        lax.all_gather(ham_index, "row", axis=0, tiled=True),
        column_vals,
        column_index,
    )

    def select_row(row_item):
        return pick_image(row_item[0], row_item[1], products, offset)

    chosen_all = initial + lax.map(select_row, (slab_where, column_pos))

    def finish_row(row_item):
        return contract_row(row_item[0], row_item[1].astype(jnp.bfloat16))

    result = lax.map(finish_row, (slab_vals, chosen_all))
    return result.astype(jnp.bfloat16)


def solution(mesh):
    placed = (
        P("row", None, None, None),
        P("row", None),
        P("col", "row", None, None),
        P("col", "row"),
        P("row", "col", None, None),
        P("row", "col"),
        P("row", "col"),
    )
    return jax.shard_map(
        shards, mesh=mesh, in_specs=placed, out_specs=P("row", "col", None, None), check_vma=False
    )
```

profile of v0, /device:TPU:1, one launch (start us, length us, event | category | flops | bytes accessed | tf_op | source)
XLA Modules:
  0.0 392.7 jit_solution(10934278853441092370)
XLA Ops:
  8.0 30.5 %all-gather = s32[16,1,4]{2,1,0:T(1,128)S(1)} all-gather(s32[1,1,4]{2,1,0:T(1,128)} %bitcast.93), channel_id=1, replica_groups=mesh['row'=16,'col'=16] {'row'}, dimensions={0}, use_global_device_ids=true | all-gather | bytes 272 | tf_op jit(solution)/shard_map/all_gather | solution.py:38
  38.6 34.4 %all_gather.23 = bf16[1,16,128,128]{3,2,0,1:T(8,128)(2,1)S(1)} all-gather(bf16[1,1,128,128]{3,2,0,1:T(8,128)(2,1)} %bitcast.91), channel_id=1, replica_groups=mesh['row'=16,'col'=16] {'col'}, dimensions={1}, use_global_device_ids=true | all-gather | bytes 557056 | tf_op jit(solution)/shard_map/all_gather | solution.py:41
  74.1 1.3 dynamic-slice.5
  76.0 6.4 %all-reduce = s32[16]{0:T(128)S(1)} all-reduce(s32[16]{0:T(128)S(1)} %bitcast_dynamic-update-slice_fusion.1), channel_id=1, replica_groups=mesh['row'=16,'col'=16] {'col'}, use_global_device_ids=true, to_apply=%add | all-reduce | flops 16 | bytes 128
  82.4 24.5 %all-gather.1 = s32[16,8,4]{1,2,0:T(4,128)S(1)} all-gather(s32[1,8,4]{1,2,0:T(4,128)} %bitcast.92), channel_id=1, replica_groups=mesh['row'=16,'col'=16] {'row'}, dimensions={0}, use_global_device_ids=true | all-gather | bytes 2176 | tf_op jit(solution)/shard_map/all_gather | solution.py:54
  108.2 3.0 copy.27
  111.2 157.5 %all-gather.5.cloned.1.call-done = bf16[128,4,128,128]{3,2,1,0:T(8,128)(2,1)} async-done(((bf16[8,4,128,128]{3,2,1,0:T(8,128)(2,1)}), bf16[128,4,128,128]{3,2,1,0:T(8,128)(2,1)}) %all-gather.5.cloned.1.call-update) | async-done | bytes 16777232 | tf_op jit(solution)/shard_map/all_gather | solution.py:53
  268.7 85.2 %while.3 = (s32[]{:T(128)}, bf16[16,8,128,4,128]{4,2,1,0,3:T(8,128)(2,1)}, bf16[16,8,4,128,128]{4,3,2,1,0:T(8,128)(2,1)}, s32[4,16]{1,0:T(4,128)S(1)}, s32[16,8,...) while((s32[]{:T(128)}, bf16[16,8,128,4,128]{4,2,1,0,3:T(8,128)(2,1)}, ...), condition=%wide.region_1.2_spmd, body=%wide.region_0.1_spmd.sunk | while | flops 606603264 | bytes 14680801 | solution.py:20
  268.7 1.3 convert_bitcast_fusion.2
  269.9 2.8 fusion.47
  274.0 1.3 convert_bitcast_fusion.2
  275.3 2.8 fusion.47
  279.3 1.3 convert_bitcast_fusion.2
  280.6 2.8 fusion.47
  284.6 1.3 convert_bitcast_fusion.2
  285.9 2.8 fusion.47
  290.0 1.3 convert_bitcast_fusion.2
  291.3 2.8 fusion.47
  295.3 1.3 convert_bitcast_fusion.2
  296.6 2.8 fusion.47
  300.6 1.3 convert_bitcast_fusion.2
  301.9 2.8 fusion.47
  305.9 1.3 convert_bitcast_fusion.2
  307.2 2.8 fusion.47
  311.2 1.3 convert_bitcast_fusion.2
  312.5 2.8 fusion.47
  315.3 1.3 copy_dynamic-update-slice_fusion.2
  316.6 1.3 convert_bitcast_fusion.2
  317.8 2.8 fusion.47
  321.9 1.3 convert_bitcast_fusion.2
  323.2 2.8 fusion.47
  326.0 1.3 copy_dynamic-update-slice_fusion.2
  327.2 1.3 convert_bitcast_fusion.2
  328.5 2.8 fusion.47
  332.6 1.3 convert_bitcast_fusion.2
  333.8 2.8 fusion.47
  337.9 1.3 convert_bitcast_fusion.2
  339.1 2.8 fusion.47
  343.2 1.3 convert_bitcast_fusion.2
  344.5 2.8 fusion.47
  348.5 1.3 convert_bitcast_fusion.2
  349.8 2.8 fusion.47
  352.5 1.3 copy_dynamic-update-slice_fusion.2
  353.8 12.0 %while.8 = (s32[]{:T(128)}, bf16[128,128,4,128]{3,1,0,2:T(8,128)(2,1)}, s32[2,1]{0,1:T(1,128)S(1)}, bf16[2,128,128,128]{3,2,1,0:T(8,128)(2,1)}, s32[]{:T(128)}) while((s32[]{:T(128)}, bf16[128,128,4,128]{3,1,0,2:T(8,128)(2,1)}, s32[2,1]{0,1:T(1,128)S(1)}, bf16[2,128,128,128]{3,2,1,0:T(8,128)(2,1)}, s32[]{:T(128)}) %tuple.44), condition=%wide.while_cond, body=%wide.while_body.sunk | while | flops 2 | bytes 8389205 | solution.py:27
  354.4 5.5 %bitcast_dynamic-update-slice_fusion.3 = bf16[2,128,128,128]{3,2,1,0:T(8,128)(2,1)} fusion(bf16[2,128,128,128]{3,2,1,0:T(8,128)(2,1)} %get-tuple-element.190, s32[]{:T(128)S(6)} %copy.74, bf16[128,128,4,128]{3,1,0,2:T(8,128)(2,1)} %get-tuple-element.193, s32[]{:T(128)} %bitcast.87), kind=kLoop, calls=%fused_computation.15.clone.1 | loop fusion | bytes 8389124 | tf_op jit(solution)/shard_map/while/body/eval_jaxpr/jit(_take)/gather
  360.5 5.4 %bitcast_dynamic-update-slice_fusion.3 = bf16[2,128,128,128]{3,2,1,0:T(8,128)(2,1)} fusion(bf16[2,128,128,128]{3,2,1,0:T(8,128)(2,1)} %get-tuple-element.190, s32[]{:T(128)S(6)} %copy.74, bf16[128,128,4,128]{3,1,0,2:T(8,128)(2,1)} %get-tuple-element.193, s32[]{:T(128)} %bitcast.87), kind=kLoop, calls=%fused_computation.15.clone.1 | loop fusion | bytes 8389124 | tf_op jit(solution)/shard_map/while/body/eval_jaxpr/jit(_take)/gather
  365.8 7.5 %select_bitcast_fusion = bf16[128,128,2,128]{3,1,0,2:T(8,128)(2,1)} fusion(bf16[2,128,128,128]{3,2,1,0:T(8,128)(2,1)} %get-tuple-element.72, pred[2]{0:T(512)(128)(4,1)S(1)} %compare_and_fusion), kind=kLoop, calls=%fused_computation.19 | loop fusion | flops 4194304 | bytes 16777218 | tf_op jit(solution)/shard_map/while/body/eval_jaxpr/jit(_take)/select_n | solution.py:27
  373.3 11.8 %fusion.29 = bf16[1,2,128,128]{2,3,1,0:T(8,128)(2,1)S(1)} fusion(bf16[128,128,2,128]{3,1,0,2:T(8,128)(2,1)} %select_bitcast_fusion, bf16[1,16,128,128]{2,1,3,0:T(8,128)(2,1)S(1)} %copy.31, s32[16]{0:T(128)S(1)} %all-reduce), kind=kOutput, calls=%fused_computation.24 | convolution fusion | flops 268994560 | bytes 8978496 | tf_op jit(solution)/shard_map/while/body/eval_jaxpr/mab,mbkc->kac/dot_general | solution.py:32
  (45 shorter events, 22.0 us)
Async XLA Ops:
  6.5 101.7 %all-gather.7.cloned.1.call-start = ((), (), s32[]{:S(2)}) async-start(), calls=%async_computation.1 | async-start | bytes 2228224 | tf_op jit(solution)/shard_map/all_gather | solution.py:37
  7.3 261.4 %all-gather.5.cloned.1.call-start = ((), (), s32[]{:S(2)}) async-start(), calls=%async_computation | async-start | bytes 17825792 | tf_op jit(solution)/shard_map/all_gather | solution.py:53
Sparse Core Ops, SparseCore 0:
  9.1 65.0 all-gather.6
  76.0 192.6 all-gather.4
where the time goes:
time: 394 us; the launch traced here: 393 us
  waiting for transfers between devices  159 us (40%)
  blocking collectives  95.8 us (24%)
  matrix products  76.7 us (19%)
  local copies, waits for them, and re-layouts  38.1 us (10%)
  between operations  14.1 us (4%)
  other arithmetic  8.81 us (2%)
    all_gather x1, waiting for transfers between devices, shards(): lax.all_gather(ham_blocks, 'row', axis=0, tiled=True)  157 us
    dot_general x16, matrix products, one_row(): jnp.einsum('kxb,kbja->xja', block_row, columns, preferred_element_type=jn...  44.4 us
    all_gather x1, blocking collectives, shards(): lax.all_gather(slab_blocks, 'col', axis=1, tiled=True)  34.4 us
    all_gather x1, blocking collectives, shards(): lax.all_gather(coef_index, 'row', axis=1, tiled=True)  30.5 us
    all_gather x1, blocking collectives, shards(): lax.all_gather(ham_index, 'row', axis=0, tiled=True)  24.5 us
    dot_general x16, matrix products, one_row(): jnp.einsum('kjm,jmab->kbja', matches, column_vals, preferred_element_type...  20.5 us
    dynamic_update_slice x16, local copies, waits for them, and re-layouts, panel_images(): lax.map(one_row, (ham_part, index_part), batch_size=min(8, row_total))  20 us
    gather x4, local copies, waits for them, and re-layouts  12 us
  transfers between devices with their start and end apart: 2, of which 1 were waited for; matrix products, arithmetic and copies ran while one was open for 2% of the time, Pallas kernels for 0%

commit v1 on v0

--- a/solution.py
+++ b/solution.py
@@ -2,6 +2,11 @@
 import jax.numpy as jnp
 from jax import lax
 from jax.sharding import PartitionSpec as P
+
+
+def apply_samples_all(inputs):
+    long_array = lax.all_to_all(jnp.stack([inputs] * lax.psum(1, "row"), 0), "row", 0, 0)
+    return jnp.concatenate(long_array, 1)
 
 
 def panel_images(ham_part, index_part, column_vals, column_index):
@@ -35,7 +40,7 @@
 def shards(ham_blocks, ham_index, coef_blocks, coef_index, slab_blocks, slab_index, pattern_index):
     column_vals, column_index = (
         lax.all_gather(coef_blocks, "row", axis=1, tiled=True),
-        lax.all_gather(coef_index, "row", axis=1, tiled=True),
+        apply_samples_all(coef_index),
     )
     slab_vals, slab_where = (
         lax.all_gather(slab_blocks, "col", axis=1, tiled=True),

time: 394 us -> 394 us (level)
  blocking collectives: 95.8 us -> 66.9 us
  waiting for transfers between devices: 159 us -> 176 us
  starting transfers between devices: 0.04 us -> 10.1 us
    all_gather x1 -> x0, blocking collectives: 30.5 us -> none  [shards(): lax.all_gather(coef_index, 'row', axis=1, tiled=True)]
    all_gather x1, waiting for transfers between devices: 157 us -> 175 us  [shards(): lax.all_gather(ham_blocks, 'row', axis=0, tiled=True)]
    all_to_all x0 -> x1, starting transfers between devices: none -> 10 us  [apply_samples_all(): lax.all_to_all(jnp.stack([inputs] * lax.psum(1, 'row'), 0), 'row', 0, 0)]
    all_gather x1, blocking collectives: 34.4 us -> 29.3 us  [shards(): lax.all_gather(slab_blocks, 'col', axis=1, tiled=True)]
    unnamed x1, blocking collectives: 6.41 us -> 11.3 us
  transfers between devices with their start and end apart: 2 -> 3, of which waited for: 1 -> 1; matrix products, arithmetic and copies ran while one was open for 2% -> 2% of each run, Pallas kernels for 0% -> 0%
where the time goes in v1:
time: 394 us; the launch traced here: 393 us
  waiting for transfers between devices  176 us (45%)
  matrix products  76.7 us (19%)
  blocking collectives  66.9 us (17%)
  local copies, waits for them, and re-layouts  39.4 us (10%)
  between operations  14.1 us (4%)
  starting transfers between devices  10.1 us (3%)
  other arithmetic  8.81 us (2%)
    all_gather x1, waiting for transfers between devices, shards(): lax.all_gather(ham_blocks, 'row', axis=0, tiled=True)  175 us
    dot_general x16, matrix products, one_row(): jnp.einsum('kxb,kbja->xja', block_row, columns, preferred_element_type=jn...  44.4 us
    all_gather x1, blocking collectives, shards(): lax.all_gather(slab_blocks, 'col', axis=1, tiled=True)  29.3 us
    all_gather x1, blocking collectives, shards(): lax.all_gather(ham_index, 'row', axis=0, tiled=True)  26.3 us
    dot_general x16, matrix products, one_row(): jnp.einsum('kjm,jmab->kbja', matches, column_vals, preferred_element_type...  20.5 us
    dynamic_update_slice x16, local copies, waits for them, and re-layouts, panel_images(): lax.map(one_row, (ham_part, index_part), batch_size=min(8, row_total))  20 us
    gather x4, local copies, waits for them, and re-layouts  12 us
    dot_general x1, matrix products, contract_row(): jnp.einsum('mab,mbkc->kac', coef_row, chosen, preferred_element_type=jnp....  11.8 us
  transfers between devices with their start and end apart: 3, of which 1 were waited for; matrix products, arithmetic and copies ran while one was open for 2% of the time, Pallas kernels for 0%

profile of v1, /device:TPU:1, one launch (start us, length us, event | category | flops | bytes accessed | tf_op | source)
XLA Modules:
  0.0 392.6 jit_solution(12456356302705964223)
XLA Ops:
  9.3 10.0 %all-to-all-start = ((s32[16,4,1]{1,2,0:T(1,128)}), s32[16,4,1]{1,2,0:T(1,128)S(1)}, u32[]{:S(2)}, u32[]{:S(2)}) async-start(s32[16,4,1]{1,2,0:T(1,128)} %stack.2), calls=%async_computation | async-start | bytes 16384 | tf_op jit(solution)/shard_map/all_to_all | solution.py:8
  19.3 29.3 %all_gather.19 = bf16[1,16,128,128]{3,2,0,1:T(8,128)(2,1)S(1)} all-gather(bf16[1,1,128,128]{3,2,0,1:T(8,128)(2,1)} %bitcast.92), channel_id=1, replica_groups=mesh['row'=16,'col'=16] {'col'}, dimensions={1}, use_global_device_ids=true | all-gather | bytes 557056 | tf_op jit(solution)/shard_map/all_gather | solution.py:46
  49.1 26.3 %all-gather = s32[16,8,4]{1,2,0:T(4,128)S(1)} all-gather(s32[1,8,4]{1,2,0:T(4,128)} %bitcast.94), channel_id=1, replica_groups=mesh['row'=16,'col'=16] {'row'}, dimensions={0}, use_global_device_ids=true | all-gather | bytes 2176 | tf_op jit(solution)/shard_map/all_gather | solution.py:59
  77.3 1.3 dynamic-slice.5
  79.3 11.3 %all-reduce = s32[16]{0:T(128)S(1)} all-reduce(s32[16]{0:T(128)S(1)} %bitcast_dynamic-update-slice_fusion.1), channel_id=1, replica_groups=mesh['row'=16,'col'=16] {'col'}, use_global_device_ids=true, to_apply=%add | all-reduce | flops 16 | bytes 128
  90.6 2.9 copy.25
  93.6 175.0 %all-gather.4.cloned.1.call-done = bf16[128,4,128,128]{3,2,1,0:T(8,128)(2,1)} async-done(((bf16[8,4,128,128]{3,2,1,0:T(8,128)(2,1)}), bf16[128,4,128,128]{3,2,1,0:T(8,128)(2,1)}) %all-gather.4.cloned.1.call-update) | async-done | bytes 16777232 | tf_op jit(solution)/shard_map/all_gather | solution.py:58
  268.6 85.1 %while.3 = (s32[]{:T(128)}, bf16[16,8,128,4,128]{4,2,1,0,3:T(8,128)(2,1)}, bf16[16,8,4,128,128]{4,3,2,1,0:T(8,128)(2,1)}, s32[4,16,1]{1,0,2:T(4,128)S(1)}, s32[1...) while((s32[]{:T(128)}, bf16[16,8,128,4,128]{4,2,1,0,3:T(8,128)(2,1)}, ...), condition=%wide.region_1.2_spmd, body=%wide.region_0.1_spmd.sunk | while | flops 606603264 | bytes 14680801 | solution.py:25
  268.6 1.3 convert_bitcast_fusion.2
  269.9 2.8 fusion.47
  273.9 1.3 convert_bitcast_fusion.2
  275.2 2.8 fusion.47
  278.0 1.3 copy_dynamic-update-slice_fusion.2
  279.2 1.3 convert_bitcast_fusion.2
  280.5 2.8 fusion.47
  284.6 1.3 convert_bitcast_fusion.2
  285.9 2.8 fusion.47
  289.9 1.3 convert_bitcast_fusion.2
  291.2 2.8 fusion.47
  295.2 1.3 convert_bitcast_fusion.2
  296.5 2.8 fusion.47
  300.5 1.3 convert_bitcast_fusion.2
  301.8 2.8 fusion.47
  305.8 1.3 convert_bitcast_fusion.2
  307.1 2.8 fusion.47
  311.1 1.3 convert_bitcast_fusion.2
  312.4 2.8 fusion.47
  315.2 1.3 copy_dynamic-update-slice_fusion.2
  316.5 1.3 convert_bitcast_fusion.2
  317.8 2.8 fusion.47
  321.8 1.3 convert_bitcast_fusion.2
  323.1 2.8 fusion.47
  327.1 1.3 convert_bitcast_fusion.2
  328.4 2.8 fusion.47
  332.4 1.3 convert_bitcast_fusion.2
  333.7 2.8 fusion.47
  337.7 1.3 convert_bitcast_fusion.2
  339.0 2.8 fusion.47
  343.0 1.3 convert_bitcast_fusion.2
  344.3 2.8 fusion.47
  348.4 1.3 convert_bitcast_fusion.2
  349.6 2.8 fusion.47
  352.4 1.3 copy_dynamic-update-slice_fusion.2
  353.7 12.0 %while.8 = (s32[]{:T(128)}, bf16[128,128,4,128]{3,1,0,2:T(8,128)(2,1)}, s32[2,1]{0,1:T(1,128)S(1)}, bf16[2,128,128,128]{3,2,1,0:T(8,128)(2,1)}, s32[]{:T(128)}) while((s32[]{:T(128)}, bf16[128,128,4,128]{3,1,0,2:T(8,128)(2,1)}, s32[2,1]{0,1:T(1,128)S(1)}, bf16[2,128,128,128]{3,2,1,0:T(8,128)(2,1)}, s32[]{:T(128)}) %tuple.45), condition=%wide.while_cond, body=%wide.while_body.sunk | while | flops 2 | bytes 8389205 | solution.py:32
  354.3 5.5 %bitcast_dynamic-update-slice_fusion.3 = bf16[2,128,128,128]{3,2,1,0:T(8,128)(2,1)} fusion(bf16[2,128,128,128]{3,2,1,0:T(8,128)(2,1)} %get-tuple-element.196, s32[]{:T(128)S(6)} %copy.72, bf16[128,128,4,128]{3,1,0,2:T(8,128)(2,1)} %get-tuple-element.199, s32[]{:T(128)} %bitcast.88), kind=kLoop, calls=%fused_computation.15.clone.1 | loop fusion | bytes 8389124 | tf_op jit(solution)/shard_map/while/body/eval_jaxpr/jit(_take)/gather
  360.3 5.4 %bitcast_dynamic-update-slice_fusion.3 = bf16[2,128,128,128]{3,2,1,0:T(8,128)(2,1)} fusion(bf16[2,128,128,128]{3,2,1,0:T(8,128)(2,1)} %get-tuple-element.196, s32[]{:T(128)S(6)} %copy.72, bf16[128,128,4,128]{3,1,0,2:T(8,128)(2,1)} %get-tuple-element.199, s32[]{:T(128)} %bitcast.88), kind=kLoop, calls=%fused_computation.15.clone.1 | loop fusion | bytes 8389124 | tf_op jit(solution)/shard_map/while/body/eval_jaxpr/jit(_take)/gather
  365.7 7.5 %select_bitcast_fusion = bf16[128,128,2,128]{3,1,0,2:T(8,128)(2,1)} fusion(bf16[2,128,128,128]{3,2,1,0:T(8,128)(2,1)} %get-tuple-element.72, pred[2]{0:T(512)(128)(4,1)S(1)} %compare_and_fusion), kind=kLoop, calls=%fused_computation.19 | loop fusion | flops 4194304 | bytes 16777218 | tf_op jit(solution)/shard_map/while/body/eval_jaxpr/jit(_take)/select_n | solution.py:32
  373.2 11.8 %fusion.29 = bf16[1,2,128,128]{2,3,1,0:T(8,128)(2,1)S(1)} fusion(bf16[128,128,2,128]{3,1,0,2:T(8,128)(2,1)} %select_bitcast_fusion, bf16[1,16,128,128]{2,1,3,0:T(8,128)(2,1)S(1)} %copy.29, s32[16]{0:T(128)S(1)} %all-reduce), kind=kOutput, calls=%fused_computation.24 | convolution fusion | flops 268994560 | bytes 8978496 | tf_op jit(solution)/shard_map/while/body/eval_jaxpr/mab,mbkc->kac/dot_general | solution.py:37
  (47 shorter events, 23.3 us)
Async XLA Ops:
  6.5 84.1 %all-gather.6.cloned.1.call-start = ((), (), s32[]{:S(2)}) async-start(), calls=%async_computation.2 | async-start | bytes 2228224 | tf_op jit(solution)/shard_map/all_gather | solution.py:42
  7.3 261.3 %all-gather.4.cloned.1.call-start = ((), (), s32[]{:S(2)}) async-start(), calls=%async_computation.1 | async-start | bytes 17825792 | tf_op jit(solution)/shard_map/all_gather | solution.py:58
  9.3 81.3 %all-to-all-start = ((s32[16,4,1]{1,2,0:T(1,128)}), s32[16,4,1]{1,2,0:T(1,128)S(1)}, u32[]{:S(2)}, u32[]{:S(2)}) async-start(s32[16,4,1]{1,2,0:T(1,128)} %stack.2), calls=%async_computation | async-start | bytes 16384 | tf_op jit(solution)/shard_map/all_to_all | solution.py:8
Sparse Core Ops, SparseCore 0:
  9.1 65.3 all-gather.5
  76.3 192.2 all-gather.3
